TPU v7x, 512 devices: a whole 4x4x16 slice. The times are simulated.
512 devices in a mesh: row: 32 (over y_hi, z), col: 16 (over x, y_lo, core).
Axes of the slice: x: 4, y: 4 (y_hi: 2, y_lo: 2; y = y_hi * 2 + y_lo), z: 16, core: 2. Of those that a mesh axis runs over, the one named last changes fastest.
Arguments:
- incoming_evolution_embedding: bfloat16 [64, 512, 64], P(None, 'row'), may hold values from -6 to 6
- learned_affine_stretch: float32 [64], replicated, may hold values from 0.5 to 1.5
- learned_affine_offset: float32 [64], replicated, may hold values from -3 to 3
- lefthand_mapping_tensor: bfloat16 [64, 32], replicated, may hold values from -0.75 to 0.75
- righthand_mapping_tensor: bfloat16 [64, 32], replicated, may hold values from -0.75 to 0.75
- final_outer_matrix: bfloat16 [1024, 128], replicated, may hold values from -0.1875 to 0.1875
- residue_couple_cotangent: bfloat16 [512, 512, 128], P('row', 'col'), may hold values from -6 to 6
Outputs:
- alignment_gradient: bfloat16 [64, 512, 64], P('col', 'row')
- left_weight_gradient: float32 [64, 32], replicated
- right_weight_gradient: float32 [64, 32], replicated
- output_weight_gradient: float32 [1024, 128], replicated
All inputs are finite; a program needn't handle non-finite values.
Results may differ from a plain program's by a relative error of at most 0.0064.
Values may be sent and summed in bfloat16 or wider, within the bound.
No kernel may reach another device: no remote copies, remote signals or barrier semaphores. Data moves between devices by JAX's collectives and lax.ppermute only.
A program may use at most 64 MiB of HBM per device.

v0:
```python
import math
import jax
import jax.numpy as jnp
from jax import lax
from jax.sharding import PartitionSpec as P

highest = lax.Precision.HIGHEST


def broadcast(x, axis, root):
    mine = lax.axis_index(axis) == root
    return lax.psum(jnp.where(mine, x, jnp.zeros_like(x)), axis)


def standardize_features(values, learned_affine_stretch, learned_affine_offset):
    values = values.astype(jnp.float32)
    mean_value = jnp.mean(values, -1, keepdims=True)
    centred = values - mean_value
    variance = jnp.mean(centred * centred, -1, keepdims=True)
    reciprocal_spread_std = lax.rsqrt(variance + 1e-05)
    multiplied_activations = centred * reciprocal_spread_std
    standardized_activations = (
        multiplied_activations * learned_affine_stretch + learned_affine_offset
    ).astype(jnp.bfloat16)
    return (multiplied_activations, reciprocal_spread_std, standardized_activations)


def project(standardized_activations, weight):
    array_shape = standardized_activations.shape
    flat = jnp.dot(
        standardized_activations.reshape(-1, array_shape[-1]),
        weight,
        preferred_element_type=jnp.float32,
    )
    return flat.astype(jnp.bfloat16).reshape(array_shape[:-1] + (weight.shape[1],))


def outer_block(left_block, right_matrix, grad_block, final_outer_matrix, element_number, hidden):
    rows = grad_block.shape[0]
    cols = grad_block.shape[1]
    outer = lax.dot_general(
        left_block, right_matrix, (((0,), (0,)), ((), ())), preferred_element_type=jnp.float32
    )
    outer = (outer * (1.0 / element_number)).astype(jnp.bfloat16)
    outer = (
        outer.reshape(rows, hidden, cols, hidden)
        .transpose(0, 2, 1, 3)
        .reshape(rows * cols, hidden * hidden)
    )
    flat_grad = grad_block.reshape(rows * cols, grad_block.shape[2])
    weight_term = lax.dot_general(
        outer, flat_grad, (((0,), (0,)), ((), ())), preferred_element_type=jnp.float32
    )
    outer_grad = lax.dot_general(
        flat_grad, final_outer_matrix, (((1,), (1,)), ((), ())), preferred_element_type=jnp.float32
    )
    outer_grad = outer_grad.astype(jnp.bfloat16)
    outer_grad = (
        outer_grad.reshape(rows, cols, hidden, hidden)
        .transpose(0, 2, 1, 3)
        .reshape(rows * hidden, cols * hidden)
    )
    left_term = lax.dot_general(
        outer_grad, right_matrix, (((1,), (1,)), ((), ())), preferred_element_type=jnp.float32
    )
    left_term = (
        (left_term * (1.0 / element_number))
        .reshape(rows, hidden, element_number)
        .transpose(2, 0, 1)
    )
    right_term = jnp.dot(left_block, outer_grad, preferred_element_type=jnp.float32) * (
        1.0 / element_number
    )
    return (weight_term, left_term, right_term)


def norm_gradient_pass(
    left_gradient,
    right_gradient,
    lefthand_mapping_tensor,
    righthand_mapping_tensor,
    multiplied_activations,
    reciprocal_spread_std,
    learned_affine_stretch,
):
    hidden = lefthand_mapping_tensor.shape[1]
    hidden_grad = jnp.dot(
        left_gradient.reshape(-1, hidden),
        lefthand_mapping_tensor.astype(jnp.float32).T,
        precision=highest,
    )
    hidden_grad = hidden_grad + jnp.dot(
        right_gradient.reshape(-1, hidden),
        righthand_mapping_tensor.astype(jnp.float32).T,
        precision=highest,
    )
    hidden_grad = hidden_grad.reshape(multiplied_activations.shape) * learned_affine_stretch
    mean_one = jnp.mean(hidden_grad, -1, keepdims=True)
    mean_two = jnp.mean(hidden_grad * multiplied_activations, -1, keepdims=True)
    return (
        reciprocal_spread_std * (hidden_grad - mean_one - multiplied_activations * mean_two)
    ).astype(jnp.bfloat16)


def weight_grad(standardized_activations, factor_grad):
    feature_width = standardized_activations.shape[-1]
    hidden = factor_grad.shape[-1]
    return lax.dot_general(
        standardized_activations.astype(jnp.float32).reshape(-1, feature_width),
        factor_grad.reshape(-1, hidden),
        (((0,), (0,)), ((), ())),
        precision=highest,
        preferred_element_type=jnp.float32,
    )


def on_device(
    incoming_evolution_embedding,
    learned_affine_stretch,
    learned_affine_offset,
    lefthand_mapping_tensor,
    righthand_mapping_tensor,
    final_outer_matrix,
    residue_couple_cotangent,
):
    homolog_number, residue_slices, feature_width = incoming_evolution_embedding.shape
    hidden = lefthand_mapping_tensor.shape[1]
    cohort_extent = lax.axis_size("row") // lax.axis_size("col")
    residue_position = lax.axis_index("col")
    row_index = lax.axis_index("row")
    multiplied_activations, reciprocal_spread_std, standardized_activations = standardize_features(
        incoming_evolution_embedding, learned_affine_stretch, learned_affine_offset
    )
    left_factor = project(standardized_activations, lefthand_mapping_tensor)
    divide_pieces = []
    for cohort_rank in range(cohort_extent):
        divide_pieces.append(
            broadcast(
                incoming_evolution_embedding, "row", cohort_extent * residue_position + cohort_rank
            )
        )
    fetched = jnp.concatenate(divide_pieces, 1)
    fetched_normed = standardize_features(fetched, learned_affine_stretch, learned_affine_offset)[2]
    right_cols = project(fetched_normed, righthand_mapping_tensor)
    tok_cols = right_cols.shape[1]
    right_matrix = right_cols.reshape(homolog_number, tok_cols * hidden)
    block_rows = math.gcd(residue_slices, 8)
    weight_acc = jnp.zeros((hidden * hidden, final_outer_matrix.shape[1]), jnp.float32)
    right_acc = jnp.zeros((homolog_number, tok_cols * hidden), jnp.float32)
    left_parts = []
    for offset in range(0, residue_slices, block_rows):
        left_block = left_factor[:, offset : offset + block_rows, :].reshape(
            homolog_number, block_rows * hidden
        )
        grad_block = residue_couple_cotangent[offset : offset + block_rows]
        weight_term, left_term, right_term = outer_block(
            left_block, right_matrix, grad_block, final_outer_matrix, homolog_number, hidden
        )
        weight_acc = weight_acc + weight_term
        right_acc = right_acc + right_term
        left_parts.append(left_term)
    left_partial = jnp.concatenate(left_parts, 1)
    left_gradient = lax.psum_scatter(left_partial, "col", scatter_dimension=0, tiled=True)
    seq_share = homolog_number // lax.axis_size("col")
    seq_first = residue_position * seq_share
    right_partial = right_acc.reshape(homolog_number, tok_cols, hidden)
    right_total = lax.psum(right_partial, "row")
    own_part = lax.dynamic_slice_in_dim(
        right_total, row_index % cohort_extent * residue_slices, residue_slices, 1
    )
    right_rows = broadcast(own_part, "col", row_index // cohort_extent)
    right_gradient = lax.dynamic_slice_in_dim(right_rows, seq_first, seq_share, 0)
    scaled_own_part = lax.dynamic_slice_in_dim(multiplied_activations, seq_first, seq_share, 0)
    inverse_own_scale = lax.dynamic_slice_in_dim(reciprocal_spread_std, seq_first, seq_share, 0)
    normed_own = lax.dynamic_slice_in_dim(standardized_activations, seq_first, seq_share, 0)
    alignment_gradient = norm_gradient_pass(
        left_gradient,
        right_gradient,
        lefthand_mapping_tensor,
        righthand_mapping_tensor,
        scaled_own_part,
        inverse_own_scale,
        learned_affine_stretch,
    )
    left_weight = weight_grad(normed_own, left_gradient)
    right_weight = weight_grad(normed_own, right_gradient)
    out_total, left_total, right_sum = lax.psum(
        (weight_acc, left_weight, right_weight), ("row", "col")
    )
    tokens = residue_slices * lax.axis_size("row")
    return (
        alignment_gradient,
        left_total * (1.0 / tokens),
        right_sum * (1.0 / tokens),
        out_total * (1.0 / tokens),
    )


def solution(mesh):
    in_specs = (P(None, "row", None), P(), P(), P(), P(), P(), P("row", "col", None))
    out_specs = (P("col", "row", None), P(), P(), P())
    return jax.shard_map(
        on_device, mesh=mesh, in_specs=in_specs, out_specs=out_specs, check_vma=False
    )
```

profile of v0, /device:TPU:1, one launch (start us, length us, event | category | flops | bytes accessed | tf_op | source)
XLA Modules:
  0.0 1406.3 jit_solution(8164136535824600437)
XLA Ops:
  7.2 1.8 broadcast_select_fusion.1
  9.1 1.2 convert_reduce_fusion
  10.3 1.3 fusion.9
  11.7 0.3 convolution_convert_fusion.1
  12.4 0.3 convolution_convert_fusion.2
  12.7 1.6 reshape.145
  14.2 2.1 copy.62
  16.4 3.6 reshape.146
  20.0 1.1 add_convert_fusion
  21.9 0.5 copy-done.11
  22.3 0.9 fusion.18
  23.3 1.6 reshape.149
  24.8 2.1 copy.61
  27.0 3.6 reshape.150
  31.1 1.8 copy.51
  33.0 265.5 %all-reduce.13.cloned.1.call-done = (bf16[64,16,64]{2,1,0:T(8,128)(2,1)}, bf16[64,16,64]{2,1,0:T(8,128)(2,1)}) async-done(((bf16[64,16,64]{2,1,0:T(8,128)(2,1)}, bf16[64,16,64]{2,1,0:T(8,128)(2,1)}), (bf16[64,16,64]{2,1,0:T(8,128)(2,1)}, bf16[64,16,64]{2,1,0:T(8,128)(2,1)})) %all-reduce.13.cloned.1.call-update) | async-done | bytes 262160 | tf_op jit(solution)/shard_map/psum | solution.py:12
  298.5 1.2 maximum_convert_fusion
  299.7 1.4 fusion.10
  301.2 0.6 multiply_reduce_fusion
  302.0 0.6 fusion.6
  302.8 0.3 copy.42
  303.1 0.5 reshape_reshape.3
  303.7 1.1 fusion
  304.8 1.1 fusion.1
  305.9 290.3 %all-reduce.7.cloned.1.call-done = f32[64,32,32]{2,1,0:T(8,128)} async-done(((f32[64,32,32]{2,1,0:T(8,128)}), f32[64,32,32]{2,1,0:T(8,128)}) %all-reduce.7.cloned.1.call-update) | async-done | bytes 262160 | tf_op jit(solution)/shard_map/psum | solution.py:167
  596.2 1.9 dynamic-slice_select_fusion
  598.3 2.9 reshape.160
  601.2 2.1 copy.60
  603.3 3.6 reshape.161
  606.9 1.2 fusion.19
  608.0 2.8 reshape.162
  610.9 2.1 copy.59
  613.0 3.6 reshape.163
  616.7 1.2 convolution_add_fusion
  618.7 1.0 copy.46
  619.8 129.4 %all-reduce.9.cloned.1.call-done = f32[64,16,32]{2,1,0:T(8,128)} async-done(((f32[64,16,32]{2,1,0:T(8,128)}), f32[64,16,32]{2,1,0:T(8,128)}) %all-reduce.9.cloned.1.call-update) | async-done | bytes 131088 | tf_op jit(solution)/shard_map/psum | solution.py:12
  749.2 0.8 constant_dynamic-slice_fusion
  749.9 1.0 convolution_bitcast_fusion
  750.9 470.0 %all-reduce.11.cloned.1.call-done = f32[1024,128]{1,0:T(8,128)} async-done(((f32[1024,128]{1,0:T(8,128)}), f32[1024,128]{1,0:T(8,128)}) %all-reduce.11.cloned.1.call-update) | async-done | bytes 524304 | tf_op jit(solution)/shard_map/psum | solution.py:187
  1220.9 1.9 broadcast_multiply_fusion
  1222.8 64.8 %reduce-scatter.2.cloned.1.call-done = f32[4,16,32]{2,1,0:T(8,128)} async-done(((f32[64,16,32]{2,1,0:T(8,128)}), f32[4,16,32]{2,1,0:T(8,128)}) %reduce-scatter.2.cloned.1.call-update) | async-done | bytes 8208 | tf_op jit(solution)/shard_map/reduce_scatter | solution.py:163
  1287.6 1.0 fusion.17
  1288.9 0.9 multiply_reduce_fusion.1
  1289.7 0.7 constant_dynamic-slice_fusion.1
  1290.5 1.0 convolution_bitcast_fusion.1
  1291.5 106.2 %all-reduce = (f32[64,32]{0,1:T(8,128)S(1)}, f32[64,32]{0,1:T(8,128)S(1)}) all-reduce(f32[64,32]{0,1:T(8,128)S(1)} %convolution_bitcast_fusion.1, f32[64,32]{0,1:T(8,128)S(1)} %convolution_bitcast_fusion), channel_id=1, replica_groups=mesh['row'=32,'col'=16] {'row','col'}, use_global_device_ids=true, to_apply=%region_11.12 | all-reduce | flops 4096 | bytes 32768 | tf_op jit(solution)/shard_map/psum | solution.py:187
  1397.7 0.6 broadcast_multiply_fusion.3
  1398.3 1.5 multiply_convert_fusion
  (77 shorter events, 3.7 us)
Async XLA Ops:
  7.2 4.6 copy-start
  7.2 4.5 copy-start.14
  7.2 291.3 %all-reduce.13.cloned.1.call-start = ((), (), s32[]{:S(2)}) async-start(), calls=%async_computation.5 | async-start | bytes 1048576 | tf_op jit(solution)/shard_map/psum | solution.py:12
  9.1 587.1 %all-reduce.7.cloned.1.call-start = ((), (), s32[]{:S(2)}) async-start(), calls=%async_computation.2 | async-start | bytes 2097152 | tf_op jit(solution)/shard_map/psum | solution.py:167
  11.7 8.3 copy-start.13
  11.7 0.6 copy-start.7
  11.7 0.6 copy-start.9
  16.4 3.6 copy-start.1
  16.4 3.6 copy-start.17
  16.4 3.6 copy-start.20
  16.4 4.8 copy-start.15
  21.2 0.7 copy-start.5
  21.7 0.6 copy-start.11
  27.0 3.7 copy-start.6
  32.9 269.0 %copy-start.18 = (f32[64]{0:T(128)S(1)}, f32[64]{0:T(128)}, u32[]{:S(2)}) copy-start(f32[64]{0:T(128)} %param.8) | copy-start | bytes 772
  32.9 269.0 %copy-start.21 = (f32[64]{0:T(128)S(1)}, f32[64]{0:T(128)}, u32[]{:S(2)}) copy-start(f32[64]{0:T(128)} %param.9) | copy-start | bytes 772
  33.0 716.2 %all-reduce.9.cloned.1.call-start = ((), (), s32[]{:S(2)}) async-start(), calls=%async_computation.3 | async-start | bytes 1048576 | tf_op jit(solution)/shard_map/psum | solution.py:12
  298.5 2.6 copy-start.2
  298.5 2.6 copy-start.3
  298.5 4.1 copy-start.16
  301.1 2.5 copy-start.12
  598.1 622.8 %all-reduce.11.cloned.1.call-start = ((), (), s32[]{:S(2)}) async-start(), calls=%async_computation.4 | async-start | bytes 1048576 | tf_op jit(solution)/shard_map/psum | solution.py:187
  603.3 3.6 copy-start.10
  613.0 3.6 copy-start.4
  613.0 3.6 copy-start.8
  618.2 670.3 %copy-start.19 = (f32[64]{0:T(128)S(1)}, f32[64]{0:T(128)}, u32[]{:S(2)}) copy-start(f32[64]{0:T(128)} %param.8) | copy-start | bytes 772
  618.3 669.3 %reduce-scatter.2.cloned.1.call-start = ((), (), s32[]{:S(2)}) async-start(), calls=%async_computation.1 | async-start | bytes 557056 | tf_op jit(solution)/shard_map/reduce_scatter | solution.py:163
Sparse Core Ops, SparseCore 0:
  11.5 286.9 all-reduce.12
  301.4 294.7 all-reduce.6
  599.7 149.4 all-reduce.8
  754.5 466.3 all-reduce.10
  1223.5 64.0 reduce-scatter.1
where the time goes:
time: 1410 us
  waiting for transfers between devices  1220 us (87%)
  blocking collectives  106 us (8%)
  local copies, waits for them, and re-layouts  38.3 us (3%)
  other arithmetic  16.7 us (1%)
  between operations  14.3 us (1%)
    psum x1, waiting for transfers between devices, on_device(): lax.psum((weight_acc, left_weight, right_weight), ('row', 'col'))  470 us
    psum x2, waiting for transfers between devices, broadcast(): return lax.psum(jnp.where(mine, x, jnp.zeros_like(x)), axis)  395 us
    psum x1, waiting for transfers between devices, on_device(): right_total = lax.psum(right_partial, 'row')  290 us
    psum x1, blocking collectives, on_device(): lax.psum((weight_acc, left_weight, right_weight), ('row', 'col'))  106 us
    reduce_scatter x1, waiting for transfers between devices, on_device(): lax.psum_scatter(left_partial, 'col', scatter_dimension=0, tiled=True)  64.8 us
  transfers between devices with their start and end apart: 5, of which 5 were waited for; matrix products, arithmetic and copies ran while one was open for 4% of the time, Pallas kernels for 0%

commit v1 on v0

--- a/solution.py
+++ b/solution.py
@@ -185,7 +185,7 @@
     left_weight = weight_grad(normed_own, left_gradient)
     right_weight = weight_grad(normed_own, right_gradient)
     out_total, left_total, right_sum = lax.psum(
-        (weight_acc, left_weight, right_weight), ("row", "col")
+        lax.psum((weight_acc, left_weight, right_weight), "col"), "row"
     )
     tokens = residue_slices * lax.axis_size("row")
     return (

time: 1410 us -> 1200 us (0.85)
  the two profiles are of different devices: /device:TPU:1 before, /device:TPU:16 now
where the time goes in v1:
time: 1200 us
  waiting for transfers between devices  913 us (76%)
  blocking collectives  203 us (17%)
  local copies, waits for them, and re-layouts  40.2 us (3%)
  other arithmetic  17.7 us (1%)
  between operations  14.3 us (1%)
    psum x2, waiting for transfers between devices, broadcast(): return lax.psum(jnp.where(mine, x, jnp.zeros_like(x)), axis)  413 us
    psum x1, waiting for transfers between devices, on_device(): right_total = lax.psum(right_partial, 'row')  303 us
    psum x1, blocking collectives, on_device(): lax.psum(lax.psum((weight_acc, left_weight, right_weight), 'col'), 'row')  147 us
    psum x1, waiting for transfers between devices, on_device(): lax.psum((weight_acc, left_weight, right_weight), 'col')  124 us
    reduce_scatter x1, waiting for transfers between devices, on_device(): lax.psum_scatter(left_partial, 'col', scatter_dimension=0, tiled=True)  72.7 us
    psum x1, blocking collectives, on_device(): lax.psum((weight_acc, left_weight, right_weight), 'col')  56.5 us
  transfers between devices with their start and end apart: 5, of which 5 were waited for; matrix products, arithmetic and copies ran while one was open for 3% of the time, Pallas kernels for 0%

profile of v1, /device:TPU:16, one launch (start us, length us, event | category | flops | bytes accessed | tf_op | source)
XLA Modules:
  0.0 1198.1 jit_solution(632864631679806659)
XLA Ops:
  7.3 1.8 broadcast_select_fusion.1
  9.2 1.2 convert_reduce_fusion
  10.4 1.3 fusion.9
  11.7 1.8 add_convert_fusion
  13.6 0.7 copy-done.3
  15.0 0.7 copy.48
  15.8 0.7 copy.49
  16.5 1.6 reshape.145
  18.1 2.2 copy.62
  20.2 3.5 reshape.146
  24.1 1.6 reshape.149
  25.7 2.2 copy.61
  27.8 3.5 reshape.150
  31.4 285.3 %all-reduce.15.cloned.1.call-done = (bf16[64,16,64]{2,1,0:T(8,128)(2,1)}, bf16[64,16,64]{2,1,0:T(8,128)(2,1)}) async-done(((bf16[64,16,64]{2,1,0:T(8,128)(2,1)}, bf16[64,16,64]{2,1,0:T(8,128)(2,1)}), (bf16[64,16,64]{2,1,0:T(8,128)(2,1)}, bf16[64,16,64]{2,1,0:T(8,128)(2,1)})) %all-reduce.15.cloned.1.call-update) | async-done | bytes 262160 | tf_op jit(solution)/shard_map/psum | solution.py:12
  316.7 1.4 fusion.10
  318.1 1.7 multiply_reduce_fusion
  319.8 1.2 maximum_convert_fusion
  321.1 0.6 fusion.6
  322.0 0.3 copy.42
  322.3 0.5 reshape_reshape.3
  322.9 1.1 fusion
  323.9 2.8 reshape.160
  326.8 2.2 copy.60
  329.0 3.7 reshape.161
  332.7 1.1 fusion.19
  333.9 1.1 fusion.1
  334.9 2.8 reshape.162
  337.8 2.2 copy.59
  339.9 3.6 reshape.163
  343.6 1.1 convolution_add_fusion
  345.6 1.0 copy.46
  347.4 1.8 copy.51
  349.2 124.1 %all-reduce.11.cloned.1.call-done = f32[1024,128]{1,0:T(8,128)} async-done(((f32[1024,128]{1,0:T(8,128)}), f32[1024,128]{1,0:T(8,128)}) %all-reduce.11.cloned.1.call-update) | async-done | bytes 524304 | tf_op jit(solution)/shard_map/psum | solution.py:188
  473.4 0.7 constant_dynamic-slice_fusion.1
  474.1 72.7 %reduce-scatter.2.cloned.1.call-done = f32[4,16,32]{2,1,0:T(8,128)} async-done(((f32[64,16,32]{2,1,0:T(8,128)}), f32[4,16,32]{2,1,0:T(8,128)}) %reduce-scatter.2.cloned.1.call-update) | async-done | bytes 8208 | tf_op jit(solution)/shard_map/reduce_scatter | solution.py:163
  546.8 1.0 convolution_bitcast_fusion.1
  547.8 1.0 fusion.17
  548.8 303.3 %all-reduce.13.cloned.1.call-done = (f32[64,32,32]{2,1,0:T(8,128)}, f32[1024,128]{1,0:T(8,128)}) async-done(((f32[64,32,32]{2,1,0:T(8,128)}, f32[1024,128]{1,0:T(8,128)}), (f32[64,32,32]{2,1,0:T(8,128)}, f32[1024,128]{1,0:T(8,128)})) %all-reduce.13.cloned.1.call-update) | async-done | bytes 786448 | tf_op jit(solution)/shard_map/psum | solution.py:167
  852.1 1.9 dynamic-slice_select_fusion
  854.0 1.9 broadcast_multiply_fusion
  855.9 127.4 %all-reduce.9.cloned.1.call-done = f32[64,16,32]{2,1,0:T(8,128)} async-done(((f32[64,16,32]{2,1,0:T(8,128)}), f32[64,16,32]{2,1,0:T(8,128)}) %all-reduce.9.cloned.1.call-update) | async-done | bytes 131088 | tf_op jit(solution)/shard_map/psum | solution.py:12
  983.3 0.8 constant_dynamic-slice_fusion
  984.3 0.9 multiply_reduce_fusion.1
  985.3 1.0 convolution_bitcast_fusion
  986.3 56.5 %all-reduce.2 = (f32[64,32]{0,1:T(8,128)S(1)}, f32[64,32]{0,1:T(8,128)S(1)}) all-reduce(f32[64,32]{0,1:T(8,128)S(1)} %convolution_bitcast_fusion.1, f32[64,32]{0,1:T(8,128)S(1)} %convolution_bitcast_fusion), channel_id=1, replica_groups=mesh['row'=32,'col'=16] {'col'}, use_global_device_ids=true, to_apply=%region_11.12 | all-reduce | flops 4096 | bytes 32768 | tf_op jit(solution)/shard_map/psum | solution.py:188
  1042.8 146.7 %all-reduce = (f32[64,32]{0,1:T(8,128)S(1)}, f32[64,32]{0,1:T(8,128)S(1)}) all-reduce(f32[64,32]{0,1:T(8,128)S(1)} %get-tuple-element.8, f32[64,32]{0,1:T(8,128)S(1)} %get-tuple-element.9), channel_id=1, replica_groups=mesh['row'=32,'col'=16] {'row'}, use_global_device_ids=true, to_apply=%region_12.13 | all-reduce | flops 4096 | bytes 32768 | tf_op jit(solution)/shard_map/psum | solution.py:187
  1189.5 0.6 broadcast_multiply_fusion.3
  1190.1 1.5 multiply_convert_fusion
  (73 shorter events, 3.6 us)
Async XLA Ops:
  7.2 7.5 copy-start
  7.2 4.5 copy-start.1
  7.2 7.0 copy-start.14
  7.2 7.4 copy-start.13
  7.2 309.5 %all-reduce.15.cloned.1.call-start = ((), (), s32[]{:S(2)}) async-start(), calls=%async_computation.5 | async-start | bytes 1048576 | tf_op jit(solution)/shard_map/psum | solution.py:12
  9.1 464.2 %all-reduce.11.cloned.1.call-start = ((), (), s32[]{:S(2)}) async-start(), calls=%async_computation.3 | async-start | bytes 1048576 | tf_op jit(solution)/shard_map/psum | solution.py:188
  11.7 1.8 copy-start.12
  13.5 0.7 copy-start.3
  14.6 3.4 copy-start.8
  14.7 9.1 copy-start.6
  31.4 289.7 %copy-start.16 = (f32[64]{0:T(128)S(1)}, f32[64]{0:T(128)}, u32[]{:S(2)}) copy-start(f32[64]{0:T(128)} %param.8) | copy-start | bytes 772
  31.4 289.7 %copy-start.18 = (f32[64]{0:T(128)S(1)}, f32[64]{0:T(128)}, u32[]{:S(2)}) copy-start(f32[64]{0:T(128)} %param.9) | copy-start | bytes 772
  318.1 3.7 copy-start.15
  321.0 1.8 copy-start.10
  328.9 3.8 copy-start.9
  329.0 4.9 copy-start.4
  339.9 3.6 copy-start.2
  339.9 3.6 copy-start.7
  344.7 2.0 copy-start.11
  344.7 2.2 copy-start.5
  344.7 202.1 %reduce-scatter.2.cloned.1.call-start = ((), (), s32[]{:S(2)}) async-start(), calls=%async_computation.1 | async-start | bytes 557056 | tf_op jit(solution)/shard_map/reduce_scatter | solution.py:163
  346.7 505.4 %all-reduce.13.cloned.1.call-start = ((), (), s32[]{:S(2)}) async-start(), calls=%async_computation.4 | async-start | bytes 3145728 | tf_op jit(solution)/shard_map/psum | solution.py:167
  473.3 510.7 %copy-start.17 = (f32[64]{0:T(128)S(1)}, f32[64]{0:T(128)}, u32[]{:S(2)}) copy-start(f32[64]{0:T(128)} %param.8) | copy-start | bytes 772
  473.4 509.9 %all-reduce.9.cloned.1.call-start = ((), (), s32[]{:S(2)}) async-start(), calls=%async_computation.2 | async-start | bytes 1048576 | tf_op jit(solution)/shard_map/psum | solution.py:12
Sparse Core Ops, SparseCore 0:
  11.5 305.1 all-reduce.14
  344.8 128.4 all-reduce.10
  476.7 70.0 reduce-scatter.1
  549.6 302.4 all-reduce.12
  854.8 128.3 all-reduce.8
